TPU v7x, 32 devices: a whole 2x2x4 slice. The times are simulated.
32 devices in a mesh: groups: 2 (over y), gx: 4 (over z), gy: 2 (over x), gz: 2 (over core).
Axes of the slice: x: 2, y: 2, z: 4, core: 2. Of those that a mesh axis runs over, the one named last changes fastest.
Arguments:
- charge: float32 [128, 64, 256], P(('groups', 'gx'), 'gy', 'gz'), parts along dimension 0, may hold values from -6 to 6
Outputs:
- potential: float32 [128, 64, 256], P(('groups', 'gx'), 'gy', 'gz'), parts along dimension 0
There are 2 independent parts, one for each index of `groups`. A program takes and returns all parts, laid end to end along the dimension named above; each array names one. Nothing has to cross between parts.
All inputs are finite; a program needn't handle non-finite values.
Results may differ from a plain program's by a relative error of at most 0.0001.
Values sent between devices are 32-bit elements; how exact they have to be, the bound alone decides.
A program may use at most 128 MiB of HBM per device.

v0:
```python
import jax
import jax.numpy as jnp
from jax import lax
from jax.sharding import PartitionSpec as P

CYCLES = 2
SWEEPS = 2
SLEV = 4
RLEV = 3


OMEGA = 2.0 / 3.0
SCREEN = 0.001


def extended(value, sides, width):
    for axis, dim in sides:
        size, length = (lax.axis_size(axis), value.shape[dim])
        up = [(i, (i + 1) % size) for i in range(size)]
        down = [(j, i) for i, j in up]
        last = lax.slice_in_dim(value, length - width, length, axis=dim)
        leading = lax.slice_in_dim(value, 0, width, axis=dim)
        before = lax.ppermute(last, axis, up)
        after = lax.ppermute(leading, axis, down)
        value = jnp.concatenate([before, value, after], axis=dim)
    return value


def operate(field, scale):
    beside_all = jnp.roll(field, 1, 0) + jnp.roll(field, -1, 0)
    beside_all = beside_all + jnp.roll(field, 1, 1) + jnp.roll(field, -1, 1)
    beside_all = beside_all + jnp.roll(field, 1, 2) + jnp.roll(field, -1, 2)
    return (6.0 * field - beside_all) * scale + SCREEN * field


def relax(field, source, scale):
    return field + OMEGA * (source - operate(field, scale)) / (6.0 * scale + SCREEN)


def restrict(field):
    size_x, size_y, size_z = field.shape
    blocks = field.reshape(size_x // 2, 2, size_y // 2, 2, size_z // 2, 2)
    return blocks.mean(axis=(1, 3, 5))


def prolong(field):
    return jnp.repeat(jnp.repeat(jnp.repeat(field, 2, 0), 2, 1), 2, 2)


def whole_cycle(level, source, field):
    scale = 0.25**level
    for sweep in range(SWEEPS):
        field = relax(field, source, scale)
    if level == SLEV + RLEV - 1:
        return field
    residual = source - operate(field, scale)
    coarse_rhs = restrict(residual)
    correction = whole_cycle(level + 1, coarse_rhs, jnp.zeros(coarse_rhs.shape, jnp.float32))
    field = field + prolong(correction)
    for sweep in range(SWEEPS):
        field = relax(field, source, scale)
    return field


def padded_apply(padded, scale):
    field = padded[1:-1, 1:-1, 1:-1]
    beside_all = padded[:-2, 1:-1, 1:-1] + padded[2:, 1:-1, 1:-1]
    beside_all = beside_all + padded[1:-1, :-2, 1:-1] + padded[1:-1, 2:, 1:-1]
    beside_all = beside_all + padded[1:-1, 1:-1, :-2] + padded[1:-1, 1:-1, 2:]
    return (6.0 * field - beside_all) * scale + SCREEN * field


def widen(field):
    return extended(field, (("gx", 0), ("gy", 1), ("gz", 2)), 1)


def spread_source(source):
    return extended(source, (("gx", 0), ("gy", 1), ("gz", 2)), 2)


def split_depth():
    return SLEV


def smooth(field, source, wide_source, scale):
    diagonal = 6.0 * scale + SCREEN
    wide_field = extended(field, (("gx", 0), ("gy", 1), ("gz", 2)), 2)
    first = (
        wide_field[1:-1, 1:-1, 1:-1]
        + OMEGA * (wide_source[1:-1, 1:-1, 1:-1] - padded_apply(wide_field, scale)) / diagonal
    )
    field = first[1:-1, 1:-1, 1:-1] + OMEGA * (source - padded_apply(first, scale)) / diagonal
    return field


def collect(block):
    slab = lax.all_gather(block, "gz", axis=2, tiled=True)
    slab = lax.all_gather(slab, "gy", axis=1, tiled=True)
    return lax.all_gather(slab, "gx", axis=0, tiled=True)


def shard_cycle(level, source, field, wide_source, depth):
    scale = 0.25**level
    field = smooth(field, source, wide_source, scale)
    residual = source - padded_apply(widen(field), scale)
    coarse_rhs = restrict(residual)
    if level + 1 < depth:
        coarse_wide = spread_source(coarse_rhs)
        correction = shard_cycle(
            level + 1, coarse_rhs, jnp.zeros(coarse_rhs.shape, jnp.float32), coarse_wide, depth
        )
    else:
        whole = collect(coarse_rhs)
        solved = whole_cycle(level + 1, whole, jnp.zeros(whole.shape, jnp.float32))
        size_x, size_y, size_z = coarse_rhs.shape
        start_x = lax.axis_index("gx") * size_x
        start_y = lax.axis_index("gy") * size_y
        start_z = lax.axis_index("gz") * size_z
        correction = lax.dynamic_slice(
            solved, (start_x, start_y, start_z), (size_x, size_y, size_z)
        )
    field = field + prolong(correction)
    return smooth(field, source, wide_source, scale)


def local(charge):
    depth = split_depth()
    potential = jnp.zeros(charge.shape, jnp.float32)
    wide_charge = spread_source(charge)
    for turn in range(CYCLES):
        potential = shard_cycle(0, charge, potential, wide_charge, depth)
    return potential


def solution(mesh):
    return jax.shard_map(
        local,
        mesh=mesh,
        in_specs=(P(("groups", "gx"), "gy", "gz"),),
        out_specs=P(("groups", "gx"), "gy", "gz"),
        check_vma=False,
    )
```

profile of v0, /device:TPU:0, one launch (start us, length us, event | category | flops | bytes accessed | tf_op | source)
XLA Modules:
  0.0 534.8 jit_solution(10717102478276733900)
XLA Ops:
  0.0 3.1 collective-permute-start
  5.2 3.8 collective-permute-start.31
  13.7 3.8 collective-permute-start.13
  17.6 3.9 collective-permute-start.7
  37.8 4.1 fusion.26
  44.7 3.8 collective-permute-start.19
  62.7 2.1 pad_maximum_fusion.46
  64.9 2.3 copy.679
  67.2 2.4 copy.681
  71.1 5.0 fusion.58
  77.7 18.1 %reshape.206 = f32[8,2,16,2,64,2]{5,4,3,2,1,0:T(8,128)} reshape(f32[16,32,128]{2,1,0:T(8,128)S(1)} %copy.557) | data formatting | bytes 524288 | tf_op jit(solution)/shard_map/reshape | solution.py:42
  95.8 7.0 %reduce_sum.136 = f32[8,16,64]{2,1,0:T(8,128)S(1)} reduce(f32[8,2,16,2,64,2]{5,4,3,2,1,0:T(8,128)} %reshape.206, f32[]{:T(128)} %constant.231.clone.1), dimensions={1,3,5}, to_apply=%region_0.0 | reduce | flops 57344 | bytes 294916 | tf_op jit(solution)/shard_map/reduce_sum | solution.py:43
  118.6 3.9 collective-permute-start.37
  130.6 3.5 reshape.207
  137.1 2.8 collective-permute-start.43
  150.1 3.1 collective-permute-start.55
  164.4 2.7 collective-permute-start.61
  177.6 2.7 collective-permute-start.67
  190.2 4.2 all-gather.7
  194.4 12.1 %all-gather.8 = f32[4,4,16]{2,1,0:T(4,128)S(1)} all-gather(f32[1,4,16]{2,1,0:T(4,128)S(1)} %bitcast.114), channel_id=4, replica_groups=mesh['groups'=2,'gx'=4,'gy'=2,'gz'=2] {'gx'}, dimensions={0}, use_global_device_ids=true | all-gather | bytes 1280 | tf_op jit(solution)/shard_map/all_gather | solution.py:99
  227.1 3.8 collective-permute-start.79
  240.7 2.8 collective-permute-start.85
  256.6 2.8 collective-permute-start.91
  261.0 2.6 collective-permute-done.90
  275.5 4.1 fusion.19
  284.5 2.4 collective-permute-start.97
  288.5 3.0 collective-permute-done.96
  303.1 4.1 fusion.12
  310.7 3.4 collective-permute-start.103
  325.3 2.1 pad_maximum_fusion.30
  327.4 2.4 copy.700
  332.7 5.0 fusion.40
  339.3 18.1 %reshape.222 = f32[8,2,16,2,64,2]{5,4,3,2,1,0:T(8,128)} reshape(f32[16,32,128]{2,1,0:T(8,128)S(1)} %copy.631) | data formatting | bytes 524288 | tf_op jit(solution)/shard_map/reshape | solution.py:42
  357.4 7.0 %reduce_sum.146 = f32[8,16,64]{2,1,0:T(8,128)S(1)} reduce(f32[8,2,16,2,64,2]{5,4,3,2,1,0:T(8,128)} %reshape.222, f32[]{:T(128)} %constant.231.clone.1), dimensions={1,3,5}, to_apply=%region_8.9 | reduce | flops 57344 | bytes 294916 | tf_op jit(solution)/shard_map/reduce_sum | solution.py:43
  365.4 3.0 collective-permute-start.109
  377.8 3.2 collective-permute-start.115
  389.3 3.5 reshape.223
  395.7 2.9 collective-permute-start.121
  408.0 2.7 collective-permute-start.127
  420.1 2.7 collective-permute-start.133
  432.0 2.9 collective-permute-start.139
  444.5 4.2 all-gather.10
  448.8 12.3 %all-gather.11 = f32[4,4,16]{2,1,0:T(4,128)S(1)} all-gather(f32[1,4,16]{2,1,0:T(4,128)S(1)} %bitcast.116), channel_id=7, replica_groups=mesh['groups'=2,'gx'=4,'gy'=2,'gz'=2] {'gx'}, dimensions={0}, use_global_device_ids=true | all-gather | bytes 1280 | tf_op jit(solution)/shard_map/all_gather | solution.py:99
  479.1 3.8 collective-permute-start.151
  492.7 2.8 collective-permute-start.157
  508.6 2.7 collective-permute-start.163
  512.9 2.8 collective-permute-done.162
  527.3 4.1 fusion.5
  (845 shorter events, 320.0 us)
Async XLA Ops:
  0.0 17.6 %collective-permute-start = (f32[2,32,128]{2,1,0:T(8,128)S(1)}, f32[2,32,128]{2,1,0:T(8,128)S(1)}, u32[]{:S(2)}, u32[]{:S(2)}) collective-permute-start(f32[2,32,128]{2,1,0:T(8,128)S(1)} %broadcast.421), channel_id=1, source_target_pairs={{0,4},{4,8},{8,12},{12,0},{1,5},{5,9},{9,13},{13,1},{2,6},{6,10},{... | collective-permute-start | bytes 98312 | tf_op jit(solution)/shard_map/ppermute | solution.py:23
  3.1 18.3 %collective-permute-start.1 = (f32[2,32,128]{2,1,0:T(8,128)S(1)}, f32[2,32,128]{2,1,0:T(8,128)S(1)}, u32[]{:S(2)}, u32[]{:S(2)}) collective-permute-start(f32[2,32,128]{2,1,0:T(8,128)S(1)} %broadcast.421), channel_id=1, source_target_pairs={{4,0},{8,4},{12,8},{0,12},{5,1},{9,5},{13,9},{1,13},{6,2},{10,6},{... | collective-permute-start | bytes 98312 | tf_op jit(solution)/shard_map/ppermute | solution.py:24
  5.2 8.5 %collective-permute-start.30 = (f32[2,8,32]{2,1,0:T(8,128)S(1)}, f32[2,8,32]{2,1,0:T(8,128)S(1)}, u32[]{:S(2)}, u32[]{:S(2)}) collective-permute-start(f32[2,8,32]{2,1,0:T(8,128)S(1)} %broadcast.435), channel_id=1, source_target_pairs={{0,4},{4,8},{8,12},{12,0},{1,5},{5,9},{9,13},{13,1},{2,6},{6,10},{... | collective-permute-start | bytes 6152 | tf_op jit(solution)/shard_map/ppermute | solution.py:23
  5.2 12.3 %collective-permute-start.31 = (f32[2,8,32]{2,1,0:T(8,128)S(1)}, f32[2,8,32]{2,1,0:T(8,128)S(1)}, u32[]{:S(2)}, u32[]{:S(2)}) collective-permute-start(f32[2,8,32]{2,1,0:T(8,128)S(1)} %broadcast.435), channel_id=1, source_target_pairs={{4,0},{8,4},{12,8},{0,12},{5,1},{9,5},{13,9},{1,13},{6,2},{10,6},{... | collective-permute-start | bytes 6152 | tf_op jit(solution)/shard_map/ppermute | solution.py:24
  9.6 43.7 %collective-permute-start.12 = (f32[2,16,64]{2,1,0:T(8,128)}, f32[2,16,64]{2,1,0:T(8,128)S(1)}, u32[]{:S(2)}, u32[]{:S(2)}) collective-permute-start(f32[2,16,64]{2,1,0:T(8,128)} %broadcast.426), channel_id=1, source_target_pairs={{0,4},{4,8},{8,12},{12,0},{1,5},{5,9},{9,13},{13,1},{2,6},{6,10},{... | collective-permute-start | bytes 24584 | tf_op jit(solution)/shard_map/ppermute | solution.py:23
  13.7 40.3 %collective-permute-start.13 = (f32[2,16,64]{2,1,0:T(8,128)}, f32[2,16,64]{2,1,0:T(8,128)S(1)}, u32[]{:S(2)}, u32[]{:S(2)}) collective-permute-start(f32[2,16,64]{2,1,0:T(8,128)} %broadcast.426), channel_id=1, source_target_pairs={{4,0},{8,4},{12,8},{0,12},{5,1},{9,5},{13,9},{1,13},{6,2},{10,6},{... | collective-permute-start | bytes 24584 | tf_op jit(solution)/shard_map/ppermute | solution.py:24
  17.5 5.7 %collective-permute-start.6 = (f32[2,32,128]{2,1,0:T(8,128)S(1)}, f32[2,32,128]{2,1,0:T(8,128)S(1)}, u32[]{:S(2)}, u32[]{:S(2)}) collective-permute-start(f32[2,32,128]{2,1,0:T(8,128)S(1)} %get-tuple-element.66), channel_id=1, source_target_pairs={{0,4},{4,8},{8,12},{12,0},{1,5},{5,9},{9,13},{13,1},{2,6},{6,10},{... | collective-permute-start | bytes 98312 | tf_op jit(solution)/shard_map/ppermute | solution.py:23
  17.6 7.3 %collective-permute-start.7 = (f32[2,32,128]{2,1,0:T(8,128)S(1)}, f32[2,32,128]{2,1,0:T(8,128)S(1)}, u32[]{:S(2)}, u32[]{:S(2)}) collective-permute-start(f32[2,32,128]{2,1,0:T(8,128)S(1)} %get-tuple-element.65), channel_id=1, source_target_pairs={{4,0},{8,4},{12,8},{0,12},{5,1},{9,5},{13,9},{1,13},{6,2},{10,6},{... | collective-permute-start | bytes 98312 | tf_op jit(solution)/shard_map/ppermute | solution.py:24
  21.5 131.8 %collective-permute-start.48 = (f32[2,4,16]{2,1,0:T(4,128)S(1)}, f32[2,4,16]{2,1,0:T(4,128)S(1)}, u32[]{:S(2)}, u32[]{:S(2)}) collective-permute-start(f32[2,4,16]{2,1,0:T(4,128)S(1)} %broadcast.444), channel_id=1, source_target_pairs={{0,4},{4,8},{8,12},{12,0},{1,5},{5,9},{9,13},{13,1},{2,6},{6,10},{... | collective-permute-start | bytes 1544 | tf_op jit(solution)/shard_map/ppermute | solution.py:23
  44.7 6.8 %collective-permute-start.18 = (f32[1,32,128]{1,0,2:T(1,128)S(1)}, f32[1,32,128]{1,0,2:T(1,128)S(1)}, u32[]{:S(2)}, u32[]{:S(2)}) collective-permute-start(f32[1,32,128]{1,0,2:T(1,128)S(1)} %get-tuple-element.39), channel_id=1, source_target_pairs={{0,4},{4,8},{8,12},{12,0},{1,5},{5,9},{9,13},{13,1},{2,6},{6,10},{... | collective-permute-start | bytes 49160 | tf_op jit(solution)/shard_map/ppermute | solution.py:23
  44.7 7.0 %collective-permute-start.19 = (f32[1,32,128]{1,0,2:T(1,128)S(1)}, f32[1,32,128]{1,0,2:T(1,128)S(1)}, u32[]{:S(2)}, u32[]{:S(2)}) collective-permute-start(f32[1,32,128]{1,0,2:T(1,128)S(1)} %get-tuple-element.40), channel_id=1, source_target_pairs={{4,0},{8,4},{12,8},{0,12},{5,1},{9,5},{13,9},{1,13},{6,2},{10,6},{... | collective-permute-start | bytes 49160 | tf_op jit(solution)/shard_map/ppermute | solution.py:24
  51.5 101.7 %collective-permute-start.49 = (f32[2,4,16]{2,1,0:T(4,128)S(1)}, f32[2,4,16]{2,1,0:T(4,128)}, u32[]{:S(2)}, u32[]{:S(2)}) collective-permute-start(f32[2,4,16]{2,1,0:T(4,128)S(1)} %broadcast.444), channel_id=1, source_target_pairs={{4,0},{8,4},{12,8},{0,12},{5,1},{9,5},{13,9},{1,13},{6,2},{10,6},{... | collective-permute-start | bytes 1544 | tf_op jit(solution)/shard_map/ppermute | solution.py:24
  51.8 66.8 %collective-permute-start.32 = (f32[8,2,32]{2,1,0:T(2,128)}, f32[8,2,32]{2,1,0:T(2,128)}, u32[]{:S(2)}, u32[]{:S(2)}) collective-permute-start(f32[8,2,32]{2,1,0:T(2,128)} %get-tuple-element.251), channel_id=1, source_target_pairs={{0,2},{2,0},{1,3},{3,1},{4,6},{6,4},{5,7},{7,5},{8,10},{10,8},{9,1... | collective-permute-start | bytes 6152 | tf_op jit(solution)/shard_map/ppermute | solution.py:23
  60.7 42.2 %collective-permute-start.14 = (f32[12,2,64]{2,1,0:T(2,128)S(1)}, f32[12,2,64]{2,1,0:T(2,128)S(1)}, u32[]{:S(2)}, u32[]{:S(2)}) collective-permute-start(f32[12,2,64]{2,1,0:T(2,128)S(1)} %get-tuple-element.89), channel_id=1, source_target_pairs={{0,2},{2,0},{1,3},{3,1},{4,6},{6,4},{5,7},{7,5},{8,10},{10,8},{9,1... | collective-permute-start | bytes 18440 | tf_op jit(solution)/shard_map/ppermute | solution.py:23
  62.1 42.8 %collective-permute-start.15 = (f32[12,2,64]{2,1,0:T(2,128)S(1)}, f32[12,2,64]{2,1,0:T(2,128)S(1)}, u32[]{:S(2)}, u32[]{:S(2)}) collective-permute-start(f32[12,2,64]{2,1,0:T(2,128)S(1)} %get-tuple-element.90), channel_id=1, source_target_pairs={{2,0},{0,2},{3,1},{1,3},{6,4},{4,6},{7,5},{5,7},{10,8},{8,10},{11,... | collective-permute-start | bytes 18440 | tf_op jit(solution)/shard_map/ppermute | solution.py:24
  102.9 5.6 %collective-permute-start.24 = (f32[2,16,64]{2,1,0:T(8,128)S(1)}, f32[2,16,64]{2,1,0:T(8,128)S(1)}, u32[]{:S(2)}, u32[]{:S(2)}) collective-permute-start(f32[2,16,64]{2,1,0:T(8,128)S(1)} %get-tuple-element.105), channel_id=1, source_target_pairs={{0,4},{4,8},{8,12},{12,0},{1,5},{5,9},{9,13},{13,1},{2,6},{6,10},{... | collective-permute-start | bytes 24584 | tf_op jit(solution)/shard_map/ppermute | solution.py:23
  115.4 14.1 %collective-permute-start.33 = (f32[8,2,32]{2,1,0:T(2,128)}, f32[8,2,32]{2,1,0:T(2,128)S(1)}, u32[]{:S(2)}, u32[]{:S(2)}) collective-permute-start(f32[8,2,32]{2,1,0:T(2,128)} %get-tuple-element.250), channel_id=1, source_target_pairs={{2,0},{0,2},{3,1},{1,3},{6,4},{4,6},{7,5},{5,7},{10,8},{8,10},{11,... | collective-permute-start | bytes 6152 | tf_op jit(solution)/shard_map/ppermute | solution.py:24
  118.5 5.5 %collective-permute-start.36 = (f32[1,16,64]{2,1,0:T(8,128)S(1)}, f32[1,16,64]{2,1,0:T(8,128)S(1)}, u32[]{:S(2)}, u32[]{:S(2)}) collective-permute-start(f32[1,16,64]{2,1,0:T(8,128)S(1)} %get-tuple-element.103), channel_id=1, source_target_pairs={{0,4},{4,8},{8,12},{12,0},{1,5},{5,9},{9,13},{13,1},{2,6},{6,10},{... | collective-permute-start | bytes 12296 | tf_op jit(solution)/shard_map/ppermute | solution.py:23
  118.6 5.4 %collective-permute-start.37 = (f32[1,16,64]{2,1,0:T(8,128)S(1)}, f32[1,16,64]{2,1,0:T(8,128)S(1)}, u32[]{:S(2)}, u32[]{:S(2)}) collective-permute-start(f32[1,16,64]{2,1,0:T(8,128)S(1)} %get-tuple-element.104), channel_id=1, source_target_pairs={{4,0},{8,4},{12,8},{0,12},{5,1},{9,5},{13,9},{1,13},{6,2},{10,6},{... | collective-permute-start | bytes 12296 | tf_op jit(solution)/shard_map/ppermute | solution.py:24
  136.0 5.6 %collective-permute-start.42 = (f32[2,8,32]{2,1,0:T(8,128)S(1)}, f32[2,8,32]{2,1,0:T(8,128)S(1)}, u32[]{:S(2)}, u32[]{:S(2)}) collective-permute-start(f32[2,8,32]{2,1,0:T(8,128)S(1)} %get-tuple-element.280), channel_id=1, source_target_pairs={{0,4},{4,8},{8,12},{12,0},{1,5},{5,9},{9,13},{13,1},{2,6},{6,10},{... | collective-permute-start | bytes 6152 | tf_op jit(solution)/shard_map/ppermute | solution.py:23
  149.0 5.5 %collective-permute-start.54 = (f32[1,8,32]{2,1,0:T(8,128)S(1)}, f32[1,8,32]{2,1,0:T(8,128)S(1)}, u32[]{:S(2)}, u32[]{:S(2)}) collective-permute-start(f32[1,8,32]{2,1,0:T(8,128)S(1)} %get-tuple-element.278), channel_id=1, source_target_pairs={{0,4},{4,8},{8,12},{12,0},{1,5},{5,9},{9,13},{13,1},{2,6},{6,10},{... | collective-permute-start | bytes 3080 | tf_op jit(solution)/shard_map/ppermute | solution.py:23
  160.4 6.7 %collective-permute-start.50 = (f32[6,2,16]{2,1,0:T(2,128)}, f32[6,2,16]{2,1,0:T(2,128)S(1)}, u32[]{:S(2)}, u32[]{:S(2)}) collective-permute-start(f32[6,2,16]{2,1,0:T(2,128)} %get-tuple-element.290), channel_id=1, source_target_pairs={{0,2},{2,0},{1,3},{3,1},{4,6},{6,4},{5,7},{7,5},{8,10},{10,8},{9,1... | collective-permute-start | bytes 2312 | tf_op jit(solution)/shard_map/ppermute | solution.py:23
  161.5 5.7 %collective-permute-start.51 = (f32[6,2,16]{2,1,0:T(2,128)}, f32[6,2,16]{2,1,0:T(2,128)S(1)}, u32[]{:S(2)}, u32[]{:S(2)}) collective-permute-start(f32[6,2,16]{2,1,0:T(2,128)} %get-tuple-element.291), channel_id=1, source_target_pairs={{2,0},{0,2},{3,1},{1,3},{6,4},{4,6},{7,5},{5,7},{10,8},{8,10},{11,... | collective-permute-start | bytes 2312 | tf_op jit(solution)/shard_map/ppermute | solution.py:24
  162.9 5.7 %collective-permute-start.60 = (f32[2,4,16]{2,1,0:T(4,128)S(1)}, f32[2,4,16]{2,1,0:T(4,128)S(1)}, u32[]{:S(2)}, u32[]{:S(2)}) collective-permute-start(f32[2,4,16]{2,1,0:T(4,128)S(1)} %broadcast_multiply_fusion.7), channel_id=1, source_target_pairs={{0,4},{4,8},{8,12},{12,0},{1,5},{5,9},{9,13},{13,1},{2,6},{6,10},{... | collective-permute-start | bytes 1544 | tf_op jit(solution)/shard_map/ppermute | solution.py:23
  176.4 5.5 %collective-permute-start.66 = (f32[1,4,16]{2,1,0:T(4,128)S(1)}, f32[1,4,16]{2,1,0:T(4,128)S(1)}, u32[]{:S(2)}, u32[]{:S(2)}) collective-permute-start(f32[1,4,16]{2,1,0:T(4,128)S(1)} %get-tuple-element.298), channel_id=1, source_target_pairs={{0,4},{4,8},{8,12},{12,0},{1,5},{5,9},{9,13},{13,1},{2,6},{6,10},{... | collective-permute-start | bytes 776 | tf_op jit(solution)/shard_map/ppermute | solution.py:23
  214.8 5.4 %collective-permute-start.72 = (f32[2,4,16]{2,1,0:T(4,128)S(1)}, f32[2,4,16]{2,1,0:T(4,128)S(1)}, u32[]{:S(2)}, u32[]{:S(2)}) collective-permute-start(f32[2,4,16]{2,1,0:T(4,128)S(1)} %bitcast.96), channel_id=1, source_target_pairs={{0,4},{4,8},{8,12},{12,0},{1,5},{5,9},{9,13},{13,1},{2,6},{6,10},{... | collective-permute-start | bytes 1544 | tf_op jit(solution)/shard_map/ppermute | solution.py:23
  227.0 5.5 %collective-permute-start.78 = (f32[2,8,32]{2,1,0:T(8,128)S(1)}, f32[2,8,32]{2,1,0:T(8,128)S(1)}, u32[]{:S(2)}, u32[]{:S(2)}) collective-permute-start(f32[2,8,32]{2,1,0:T(8,128)S(1)} %get-tuple-element.274), channel_id=1, source_target_pairs={{0,4},{4,8},{8,12},{12,0},{1,5},{5,9},{9,13},{13,1},{2,6},{6,10},{... | collective-permute-start | bytes 6152 | tf_op jit(solution)/shard_map/ppermute | solution.py:23
  227.1 5.4 %collective-permute-start.79 = (f32[2,8,32]{2,1,0:T(8,128)S(1)}, f32[2,8,32]{2,1,0:T(8,128)S(1)}, u32[]{:S(2)}, u32[]{:S(2)}) collective-permute-start(f32[2,8,32]{2,1,0:T(8,128)S(1)} %get-tuple-element.275), channel_id=1, source_target_pairs={{4,0},{8,4},{12,8},{0,12},{5,1},{9,5},{13,9},{1,13},{6,2},{10,6},{... | collective-permute-start | bytes 6152 | tf_op jit(solution)/shard_map/ppermute | solution.py:24
  239.6 5.7 %collective-permute-start.84 = (f32[2,16,64]{2,1,0:T(8,128)S(1)}, f32[2,16,64]{2,1,0:T(8,128)S(1)}, u32[]{:S(2)}, u32[]{:S(2)}) collective-permute-start(f32[2,16,64]{2,1,0:T(8,128)S(1)} %get-tuple-element.101), channel_id=1, source_target_pairs={{0,4},{4,8},{8,12},{12,0},{1,5},{5,9},{9,13},{13,1},{2,6},{6,10},{... | collective-permute-start | bytes 24584 | tf_op jit(solution)/shard_map/ppermute | solution.py:23
  255.4 8.3 %collective-permute-start.90 = (f32[2,32,128]{1,0,2:T(2,128)S(1)}, f32[2,32,128]{1,0,2:T(2,128)S(1)}, u32[]{:S(2)}, u32[]{:S(2)}) collective-permute-start(f32[2,32,128]{1,0,2:T(2,128)S(1)} %get-tuple-element.37), channel_id=1, source_target_pairs={{0,4},{4,8},{8,12},{12,0},{1,5},{5,9},{9,13},{13,1},{2,6},{6,10},{... | collective-permute-start | bytes 98312 | tf_op jit(solution)/shard_map/ppermute | solution.py:23
  256.6 8.5 %collective-permute-start.91 = (f32[2,32,128]{1,0,2:T(2,128)S(1)}, f32[2,32,128]{1,0,2:T(2,128)S(1)}, u32[]{:S(2)}, u32[]{:S(2)}) collective-permute-start(f32[2,32,128]{1,0,2:T(2,128)S(1)} %get-tuple-element.38), channel_id=1, source_target_pairs={{4,0},{8,4},{12,8},{0,12},{5,1},{9,5},{13,9},{1,13},{6,2},{10,6},{... | collective-permute-start | bytes 98312 | tf_op jit(solution)/shard_map/ppermute | solution.py:24
  283.0 8.4 %collective-permute-start.96 = (f32[2,32,128]{1,0,2:T(2,128)}, f32[2,32,128]{1,0,2:T(2,128)S(1)}, u32[]{:S(2)}, u32[]{:S(2)}) collective-permute-start(f32[2,32,128]{1,0,2:T(2,128)} %get-tuple-element.35), channel_id=1, source_target_pairs={{0,4},{4,8},{8,12},{12,0},{1,5},{5,9},{9,13},{13,1},{2,6},{6,10},{... | collective-permute-start | bytes 98312 | tf_op jit(solution)/shard_map/ppermute | solution.py:23
  284.5 8.3 %collective-permute-start.97 = (f32[2,32,128]{1,0,2:T(2,128)S(1)}, f32[2,32,128]{1,0,2:T(2,128)S(1)}, u32[]{:S(2)}, u32[]{:S(2)}) collective-permute-start(f32[2,32,128]{1,0,2:T(2,128)S(1)} %get-tuple-element.36), channel_id=1, source_target_pairs={{4,0},{8,4},{12,8},{0,12},{5,1},{9,5},{13,9},{1,13},{6,2},{10,6},{... | collective-permute-start | bytes 98312 | tf_op jit(solution)/shard_map/ppermute | solution.py:24
  310.0 6.8 %collective-permute-start.102 = (f32[1,32,128]{1,0,2:T(1,128)S(1)}, f32[1,32,128]{1,0,2:T(1,128)S(1)}, u32[]{:S(2)}, u32[]{:S(2)}) collective-permute-start(f32[1,32,128]{1,0,2:T(1,128)S(1)} %get-tuple-element.33), channel_id=1, source_target_pairs={{0,4},{4,8},{8,12},{12,0},{1,5},{5,9},{9,13},{13,1},{2,6},{6,10},{... | collective-permute-start | bytes 49160 | tf_op jit(solution)/shard_map/ppermute | solution.py:23
  310.7 6.2 %collective-permute-start.103 = (f32[1,32,128]{1,0,2:T(1,128)S(1)}, f32[1,32,128]{1,0,2:T(1,128)S(1)}, u32[]{:S(2)}, u32[]{:S(2)}) collective-permute-start(f32[1,32,128]{1,0,2:T(1,128)S(1)} %get-tuple-element.34), channel_id=1, source_target_pairs={{4,0},{8,4},{12,8},{0,12},{5,1},{9,5},{13,9},{1,13},{6,2},{10,6},{... | collective-permute-start | bytes 49160 | tf_op jit(solution)/shard_map/ppermute | solution.py:24
  364.5 5.7 %collective-permute-start.108 = (f32[2,16,64]{2,1,0:T(8,128)S(1)}, f32[2,16,64]{2,1,0:T(8,128)S(1)}, u32[]{:S(2)}, u32[]{:S(2)}) collective-permute-start(f32[2,16,64]{2,1,0:T(8,128)S(1)} %get-tuple-element.99), channel_id=1, source_target_pairs={{0,4},{4,8},{8,12},{12,0},{1,5},{5,9},{9,13},{13,1},{2,6},{6,10},{... | collective-permute-start | bytes 24584 | tf_op jit(solution)/shard_map/ppermute | solution.py:23
  377.2 5.5 %collective-permute-start.114 = (f32[1,16,64]{2,1,0:T(8,128)S(1)}, f32[1,16,64]{2,1,0:T(8,128)S(1)}, u32[]{:S(2)}, u32[]{:S(2)}) collective-permute-start(f32[1,16,64]{2,1,0:T(8,128)S(1)} %get-tuple-element.97), channel_id=1, source_target_pairs={{0,4},{4,8},{8,12},{12,0},{1,5},{5,9},{9,13},{13,1},{2,6},{6,10},{... | collective-permute-start | bytes 12296 | tf_op jit(solution)/shard_map/ppermute | solution.py:23
  377.8 4.8 collective-permute-start.115
  394.7 5.5 %collective-permute-start.120 = (f32[2,8,32]{2,1,0:T(8,128)S(1)}, f32[2,8,32]{2,1,0:T(8,128)S(1)}, u32[]{:S(2)}, u32[]{:S(2)}) collective-permute-start(f32[2,8,32]{2,1,0:T(8,128)S(1)} %get-tuple-element.272), channel_id=1, source_target_pairs={{0,4},{4,8},{8,12},{12,0},{1,5},{5,9},{9,13},{13,1},{2,6},{6,10},{... | collective-permute-start | bytes 6152 | tf_op jit(solution)/shard_map/ppermute | solution.py:23
  406.7 5.5 %collective-permute-start.126 = (f32[1,8,32]{2,1,0:T(8,128)S(1)}, f32[1,8,32]{2,1,0:T(8,128)S(1)}, u32[]{:S(2)}, u32[]{:S(2)}) collective-permute-start(f32[1,8,32]{2,1,0:T(8,128)S(1)} %get-tuple-element.270), channel_id=1, source_target_pairs={{0,4},{4,8},{8,12},{12,0},{1,5},{5,9},{9,13},{13,1},{2,6},{6,10},{... | collective-permute-start | bytes 3080 | tf_op jit(solution)/shard_map/ppermute | solution.py:23
  418.8 5.5 %collective-permute-start.132 = (f32[2,4,16]{2,1,0:T(4,128)S(1)}, f32[2,4,16]{2,1,0:T(4,128)S(1)}, u32[]{:S(2)}, u32[]{:S(2)}) collective-permute-start(f32[2,4,16]{2,1,0:T(4,128)S(1)} %broadcast_multiply_fusion.6), channel_id=1, source_target_pairs={{0,4},{4,8},{8,12},{12,0},{1,5},{5,9},{9,13},{13,1},{2,6},{6,10},{... | collective-permute-start | bytes 1544 | tf_op jit(solution)/shard_map/ppermute | solution.py:23
  430.7 5.5 %collective-permute-start.138 = (f32[1,4,16]{2,1,0:T(4,128)S(1)}, f32[1,4,16]{2,1,0:T(4,128)S(1)}, u32[]{:S(2)}, u32[]{:S(2)}) collective-permute-start(f32[1,4,16]{2,1,0:T(4,128)S(1)} %get-tuple-element.296), channel_id=1, source_target_pairs={{0,4},{4,8},{8,12},{12,0},{1,5},{5,9},{9,13},{13,1},{2,6},{6,10},{... | collective-permute-start | bytes 776 | tf_op jit(solution)/shard_map/ppermute | solution.py:23
  466.8 5.4 %collective-permute-start.144 = (f32[2,4,16]{2,1,0:T(4,128)S(1)}, f32[2,4,16]{2,1,0:T(4,128)S(1)}, u32[]{:S(2)}, u32[]{:S(2)}) collective-permute-start(f32[2,4,16]{2,1,0:T(4,128)S(1)} %bitcast.90), channel_id=1, source_target_pairs={{0,4},{4,8},{8,12},{12,0},{1,5},{5,9},{9,13},{13,1},{2,6},{6,10},{... | collective-permute-start | bytes 1544 | tf_op jit(solution)/shard_map/ppermute | solution.py:23
  479.0 5.5 %collective-permute-start.150 = (f32[2,8,32]{2,1,0:T(8,128)S(1)}, f32[2,8,32]{2,1,0:T(8,128)S(1)}, u32[]{:S(2)}, u32[]{:S(2)}) collective-permute-start(f32[2,8,32]{2,1,0:T(8,128)S(1)} %get-tuple-element.266), channel_id=1, source_target_pairs={{0,4},{4,8},{8,12},{12,0},{1,5},{5,9},{9,13},{13,1},{2,6},{6,10},{... | collective-permute-start | bytes 6152 | tf_op jit(solution)/shard_map/ppermute | solution.py:23
  479.1 5.4 %collective-permute-start.151 = (f32[2,8,32]{2,1,0:T(8,128)S(1)}, f32[2,8,32]{2,1,0:T(8,128)S(1)}, u32[]{:S(2)}, u32[]{:S(2)}) collective-permute-start(f32[2,8,32]{2,1,0:T(8,128)S(1)} %get-tuple-element.267), channel_id=1, source_target_pairs={{4,0},{8,4},{12,8},{0,12},{5,1},{9,5},{13,9},{1,13},{6,2},{10,6},{... | collective-permute-start | bytes 6152 | tf_op jit(solution)/shard_map/ppermute | solution.py:24
  491.6 5.7 %collective-permute-start.156 = (f32[2,16,64]{2,1,0:T(8,128)S(1)}, f32[2,16,64]{2,1,0:T(8,128)S(1)}, u32[]{:S(2)}, u32[]{:S(2)}) collective-permute-start(f32[2,16,64]{2,1,0:T(8,128)S(1)} %get-tuple-element.95), channel_id=1, source_target_pairs={{0,4},{4,8},{8,12},{12,0},{1,5},{5,9},{9,13},{13,1},{2,6},{6,10},{... | collective-permute-start | bytes 24584 | tf_op jit(solution)/shard_map/ppermute | solution.py:23
  507.4 8.3 %collective-permute-start.162 = (f32[2,32,128]{1,0,2:T(2,128)S(1)}, f32[2,32,128]{1,0,2:T(2,128)S(1)}, u32[]{:S(2)}, u32[]{:S(2)}) collective-permute-start(f32[2,32,128]{1,0,2:T(2,128)S(1)} %get-tuple-element.31), channel_id=1, source_target_pairs={{0,4},{4,8},{8,12},{12,0},{1,5},{5,9},{9,13},{13,1},{2,6},{6,10},{... | collective-permute-start | bytes 98312 | tf_op jit(solution)/shard_map/ppermute | solution.py:23
  508.6 8.4 %collective-permute-start.163 = (f32[2,32,128]{1,0,2:T(2,128)S(1)}, f32[2,32,128]{1,0,2:T(2,128)S(1)}, u32[]{:S(2)}, u32[]{:S(2)}) collective-permute-start(f32[2,32,128]{1,0,2:T(2,128)S(1)} %get-tuple-element.32), channel_id=1, source_target_pairs={{4,0},{8,4},{12,8},{0,12},{5,1},{9,5},{13,9},{1,13},{6,2},{10,6},{... | collective-permute-start | bytes 98312 | tf_op jit(solution)/shard_map/ppermute | solution.py:24
  (165 other events, 1046.0 us)
where the time goes:
time: 542 us; the launch traced here: 535 us
  starting transfers between devices  180 us (33%)
  waiting for transfers between devices  124 us (23%)
  local copies, waits for them, and re-layouts  106 us (20%)
  other arithmetic  86 us (16%)
  blocking collectives  36.5 us (7%)
    ppermute x84, starting transfers between devices, extended(): after = lax.ppermute(leading, axis, down)  118 us
    ppermute x84, waiting for transfers between devices, extended(): before = lax.ppermute(last, axis, up)  87.8 us
    ppermute x84, starting transfers between devices, extended(): before = lax.ppermute(last, axis, up)  61.8 us
    reshape x8, local copies, waits for them, and re-layouts, restrict(): blocks = field.reshape(size_x // 2, 2, size_y // 2, 2, size_z // 2, 2)  43.8 us
    ppermute x84, waiting for transfers between devices, extended(): after = lax.ppermute(leading, axis, down)  35.9 us
    all_gather x2, blocking collectives, collect(): return lax.all_gather(slab, 'gx', axis=0, tiled=True)  24.5 us
    unnamed x119, local copies, waits for them, and re-layouts  23.4 us
    add x16, other arithmetic, smooth(): wide_field[1:-1, 1:-1, 1:-1]  21.9 us
  transfers between devices with their start and end apart: 168, of which 122 were waited for; matrix products, arithmetic and copies ran while one was open for 15% of the time, Pallas kernels for 0%

commit v1 on v0

v1 whole, which is shorter than its diff:
```python
import functools

import jax
import jax.numpy as jnp
from jax import lax
from jax.experimental import pallas as pl
from jax.experimental.pallas import tpu as pltpu
from jax.sharding import PartitionSpec as P

CYCLES = 2
LEVELS = 7

OMEGA = 2.0 / 3.0
SCREEN = 0.001

HALO = 8
SENT = 7
ROWS = 8
WIDE = 8
LANES = 128
MESH = pl.DeviceIdType.MESH


def factors(level):
    scale = 0.25**level
    diagonal = 6.0 * scale + SCREEN
    return scale, diagonal, OMEGA / diagonal, OMEGA * scale / diagonal


def roll(value, shift, axis):
    size = value.shape[axis]
    return value if size == 1 else pltpu.roll(value, shift % size, axis)


def split_dot(value, matrix):
    high = value.astype(jnp.bfloat16)
    low = (value - high.astype(jnp.float32)).astype(jnp.bfloat16)
    dot = functools.partial(jnp.dot, preferred_element_type=jnp.float32)
    return dot(high, matrix) + dot(low, matrix)


def dot_lanes(value, matrix):
    shape = value.shape
    out = split_dot(value.reshape(-1, shape[-1]), matrix)
    return out.reshape(shape[:-1] + (matrix.shape[-1],))


def indicator(rows, columns, rule):
    i = lax.broadcasted_iota(jnp.int32, (rows, columns), 0)
    j = lax.broadcasted_iota(jnp.int32, (rows, columns), 1)
    return jnp.where(rule(i, j), 1.0, 0.0).astype(jnp.bfloat16)


def plane_sum(value):
    last = value.ndim - 1
    total = roll(value, 1, last - 1) + roll(value, -1, last - 1)
    return total + (roll(value, 1, last) + roll(value, -1, last))


def inner_sum(value):
    return value[:-2] + value[2:] + plane_sum(value[1:-1])


def wrap_sum(value):
    if value.shape[0] == 1:
        beside = value + value
    else:
        beside = jnp.concatenate([value[-1:], value[:-1]], 0) + jnp.concatenate([value[1:], value[:1]], 0)
    return beside + plane_sum(value)


def kernel(sizes, charge_ref, out_ref, raw, src, va, vb, pairs, tall, f1_local, f1, v1, w1, sum1, slots,
           chunks, window, mats, split_mat, join_mat, staged, *rest):
    n_gx, n_gy, n_gz = sizes
    n_levels = LEVELS - 2
    fs, vs, ts, us = (rest[k * n_levels:(k + 1) * n_levels] for k in range(4))
    (send0, recv0, send1, recv1, send2, recv2, send3, recv3) = rest[4 * n_levels:]
    ix, iy, iz = lax.axis_index("gx"), lax.axis_index("gy"), lax.axis_index("gz")
    bx, cy, cz = charge_ref.shape
    by = cy // n_gz
    n_yb = n_gy * n_gz
    x0, r0 = bx + 2 * HALO, by + 2 * ROWS
    b1x, b1y = bx // 2, by // 2
    b2x, b2y = b1x // 2, b1y // 2
    nx2 = b2x * n_gx
    iyb = iy * n_gz + iz
    other = 1 - iz

    def place(x, yb):
        x = lax.rem(x + n_gx, n_gx)
        yb = lax.rem(yb + n_yb, n_yb)
        return {"gx": x, "gy": lax.div(yb, n_gz), "gz": lax.rem(yb, n_gz)}

    peers = [(dx, dyb) for dx in range(n_gx) for dyb in range(n_yb) if (dx, dyb) != (0, 0)]
    barrier = pltpu.get_barrier_semaphore()
    for dx, dyb in peers:
        pl.semaphore_signal(barrier, inc=1, device_id=place(ix + dx, iyb + dyb), device_id_type=MESH)
    pl.semaphore_wait(barrier, len(peers))

    first = []
    waits = []
    for k, dx in enumerate((-1, 0, 1)):
        planes = bx if dx == 0 else SENT
        from_x = 0 if dx < 1 else bx - SENT
        to_x = {-1: HALO + bx, 0: HALO, 1: HALO - SENT}[dx]
        for t, zt in enumerate((other, iz)):
            from_y = pl.multiple_of((by - ROWS) * zt, 8)
            to_y = pl.multiple_of(ROWS * (1 - zt), 8)
            source = charge_ref.at[pl.ds(from_x, planes), pl.ds(from_y, by + ROWS), :]
            target = raw.at[iz, pl.ds(to_x, planes), pl.ds(to_y, by + ROWS), :]
            if dx == 0 and t == 1:
                pltpu.make_async_copy(source, target, recv0.at[k, 0, iz]).start()
            else:
                first.append(pltpu.make_async_remote_copy(
                    src_ref=source, dst_ref=target, send_sem=send0.at[k, t], recv_sem=recv0.at[k, 0, iz],
                    device_id=place(ix + dx, iy * n_gz + zt), device_id_type=MESH))
        for t, (step, from_y, to_y) in enumerate(((-1, 0, r0 - ROWS), (n_gz, cy - ROWS, 0))):
            first.append(pltpu.make_async_remote_copy(
                src_ref=charge_ref.at[pl.ds(from_x, planes), pl.ds(from_y, ROWS), :],
                dst_ref=raw.at[iz, pl.ds(to_x, planes), pl.ds(to_y, ROWS), :],
                send_sem=send0.at[k, 2 + t], recv_sem=recv0.at[k, 1, iz],
                device_id=place(ix + dx, iy * n_gz + step), device_id_type=MESH))
        for z in range(n_gz):
            own = raw.at[z, pl.ds(to_x, planes), pl.ds(pl.multiple_of(ROWS * other, 8), by + ROWS), :]
            side = raw.at[z, pl.ds(to_x, planes), pl.ds(pl.multiple_of((r0 - ROWS) * iz, 8), ROWS), :]
            waits.append(pltpu.make_async_copy(own, own, recv0.at[k, 0, z]))
            waits.append(pltpu.make_async_copy(side, side, recv0.at[k, 1, z]))
    for copy in first:
        copy.start()

    nz = n_gz * cz
    half = nz // 2
    split_mat[...] = indicator(nz, nz, lambda i, j: i == jnp.where(j < half, 2 * j, 2 * (j - half) + 1))
    join_mat[...] = indicator(nz, nz, lambda i, j: j == jnp.where(i < half, 2 * i, 2 * (i - half) + 1))
    for level in range(1, LEVELS - 1):
        period = nz >> level
        mats[level - 1, 0] = indicator(
            LANES, LANES, lambda i, j: lax.div(i, 2) == (j & (period // 2 - 1)) + jnp.where(i < period, 0, LANES))
        mats[level - 1, 1] = indicator(LANES, LANES, lambda i, j: i == lax.div(j & (period - 1), 2))

    for wait in waits:
        wait.wait()

    filled = bx + 2 * SENT
    step = max(d for d in range(1, 7) if filled % d == 0)

    def deal(c, _):
        planes = pl.ds(HALO - SENT + step * c, step)
        value = jnp.concatenate([raw[0, planes], raw[1, planes]], -1)
        value = dot_lanes(value, split_mat[...])
        src[0, planes] = value[..., :half]
        src[1, planes] = value[..., half:]
        return _

    lax.fori_loop(0, filled // step, deal, None)

    def neighbours(ref, p):
        even, odd = ref[0, p], ref[1, p]
        rows = lambda value: roll(value, 1, 0) + roll(value, -1, 0)
        sum_even = (ref[0, p - 1] + ref[0, p + 1]) + rows(even) + (odd + roll(odd, 1, 1))
        sum_odd = (ref[1, p - 1] + ref[1, p + 1]) + rows(odd) + (even + roll(even, -1, 1))
        return (even, odd), (sum_even, sum_odd)

    def over(extent, body):
        low = HALO - extent

        def pair(c, _):
            p = low + 2 * c
            body(p, c)
            return _

        lax.fori_loop(0, (bx + 2 * extent) // 2, pair, None)

    scale0, diag0, alpha0, beta0 = factors(0)

    def begin0(ref, extent):
        def body(p, c):
            for q in (p, p + 1):
                centre, beside = neighbours(src, q)
                for z in range(2):
                    ref[z, q] = alpha0 * ((2.0 - OMEGA) * centre[z] + beta0 * beside[z])

        over(extent, body)

    def sweep0(old, new, extent):
        def body(p, c):
            for q in (p, p + 1):
                centre, beside = neighbours(old, q)
                for z in range(2):
                    new[z, q] = (1.0 - OMEGA) * centre[z] + alpha0 * src[z, q] + beta0 * beside[z]

        over(extent, body)

    def residual0(ref, extent):
        def body(p, c):
            total = None
            for q in (p, p + 1):
                centre, beside = neighbours(ref, q)
                for z in range(2):
                    term = src[z, q] - diag0 * centre[z] + scale0 * beside[z]
                    total = term if total is None else total + term
            pairs[c] = total

        over(extent, body)
        count = (bx + 2 * extent) // 2
        return 0.125 * (pairs[pl.ds(0, count), pl.ds(0, r0 // 2, stride=2), :]
                        + pairs[pl.ds(0, count), pl.ds(1, r0 // 2, stride=2), :])

    def correct0(ref, extent):
        low1 = WIDE - extent // 2 - extent % 2
        count = b1x + 2 * (WIDE - low1)
        row1 = WIDE - ROWS // 2
        value = v1[pl.ds(low1, count), pl.ds(row1, r0 // 2), :]
        tall[pl.ds(0, count), pl.ds(0, r0 // 2, stride=2), :] = value
        tall[pl.ds(0, count), pl.ds(1, r0 // 2, stride=2), :] = value
        start = HALO - 2 * (WIDE - low1)

        def body(c, _):
            term = tall[c]
            for q in range(2):
                for z in range(2):
                    ref[z, start + 2 * c + q] = ref[z, start + 2 * c + q] + term
            return _

        lax.fori_loop(0, count, body, None)

    scale1, diag1, alpha1, beta1 = factors(1)

    def span(extent):
        return slice(WIDE - extent, WIDE + b1x + extent)

    def begin1(source, extent):
        f = source[span(extent + 1)]
        return alpha1 * ((2.0 - OMEGA) * f[1:-1] + beta1 * inner_sum(f))

    def sweep1(old, source, extent):
        v = old[span(extent + 1)]
        return (1.0 - OMEGA) * v[1:-1] + alpha1 * source[span(extent)] + beta1 * inner_sum(v)

    def residual1(source):
        v = v1[span(1)]
        r = source[span(0)] - diag1 * v[1:-1] + scale1 * inner_sum(v)
        r = r.reshape((b2x, 2) + r.shape[1:]).sum(1)
        sum1[...] = r
        r = (sum1[:, pl.ds(WIDE, b2y, stride=2), :] + sum1[:, pl.ds(WIDE + 1, b2y, stride=2), :]) * 0.125
        return r

    def coarse(k):
        level = k + 2
        scale, diagonal, alpha, beta = factors(level)
        f = fs[k][...]
        v = alpha * ((2.0 - OMEGA) * f + beta * wrap_sum(f))
        if k == n_levels - 1:
            vs[k][...] = v
            return
        r = f - diagonal * v + scale * wrap_sum(v)
        vs[k][...] = v
        rows = r.shape[1]
        us[k][...] = r.reshape((r.shape[0] // 2, 2) + r.shape[1:]).sum(1)
        r = us[k][:, pl.ds(0, rows // 2, stride=2), :] + us[k][:, pl.ds(1, rows // 2, stride=2), :]
        if rows == 8:
            r = jnp.concatenate([r, r], 1)
        fs[k + 1][...] = 0.125 * dot_lanes(r, mats[level - 1, 0])
        coarse(k + 1)
        c = dot_lanes(vs[k + 1][...], mats[level - 1, 1])[:, : rows // 2]
        ts[k][:, pl.ds(0, rows // 2, stride=2), :] = c
        ts[k][:, pl.ds(1, rows // 2, stride=2), :] = c
        c = ts[k][...]
        c = jnp.broadcast_to(c[:, None], (c.shape[0], 2) + c.shape[1:]).reshape(v.shape)
        v = vs[k][...] + c
        for sweep in range(2):
            v = (1.0 - OMEGA) * v + alpha * fs[k][...] + beta * wrap_sum(v)
        vs[k][...] = v

    lane = lax.broadcasted_iota(jnp.int32, (8, LANES), 1)
    me = ix * n_yb + iyb
    begin0(va, SENT - 1)
    done = []
    for cycle in range(CYCLES):
        last = cycle == CYCLES - 1
        ahead = 4 if cycle == 0 else 0
        reach = 4 if last else 6
        rhs = residual0(va, ahead)
        low = WIDE - ahead // 2
        row1 = WIDE - ROWS // 2
        f1_here = f1.at[cycle]
        f1_here[pl.ds(WIDE, b1x), pl.ds(WIDE, b1y), :] = rhs[ahead // 2: ahead // 2 + b1x, WIDE - row1: WIDE - row1 + b1y]
        exchange = []
        for k, (dx, dy) in enumerate([(a, b) for a in (-1, 0, 1) for b in (-1, 0, 1) if (a, b) != (0, 0)]):
            planes = b1x if dx == 0 else reach
            from_x = WIDE + (b1x - reach if dx == 1 else 0)
            to_x = {-1: WIDE + b1x, 0: WIDE, 1: WIDE - reach}[dx]
            exchange.append(pltpu.make_async_remote_copy(
                src_ref=f1_here.at[pl.ds(from_x, planes), pl.ds(WIDE, b1y), :],
                dst_ref=f1_here.at[pl.ds(to_x, planes), pl.ds(WIDE - dy * b1y, b1y), :],
                send_sem=send1.at[cycle, k], recv_sem=recv1.at[cycle, k],
                device_id=place(ix + dx, iyb + dy), device_id_type=MESH))
        if cycle == 0:
            f1_local[pl.ds(low, rhs.shape[0]), pl.ds(row1, r0 // 2), :] = rhs
            down = f1_local
        else:
            for copy in exchange:
                copy.start()
            for copy in exchange:
                copy.wait_recv()
            down = f1_here
        v1[span(1)] = begin1(down, 1)
        rhs2 = dot_lanes(residual1(down).reshape(b2x * b2y, LANES), mats[0, 0])
        count = b2x * b2y // 2
        slots[cycle, me] = jnp.where(lane < LANES // 2, rhs2[:count], rhs2[count:])
        gather = []
        for k, (dx, dyb) in enumerate(peers):
            gather.append(pltpu.make_async_remote_copy(
                src_ref=slots.at[cycle, me], dst_ref=slots.at[cycle, me],
                send_sem=send2.at[cycle, k], recv_sem=recv2.at[cycle, me],
                device_id=place(ix + dx, iyb + dyb), device_id_type=MESH))
        for copy in gather:
            copy.start()
        if cycle == 0:
            for copy in exchange:
                copy.start()
        for dx, dyb in peers:
            who = lax.rem(ix + dx, n_gx) * n_yb + lax.rem(iyb + dyb, n_yb)
            slot = slots.at[cycle, who]
            pltpu.make_async_copy(slot, slot, recv2.at[cycle, who]).wait()
        for x in range(n_gx):
            for yb in range(n_yb):
                tile = slots[cycle, x * n_yb + yb]
                turned = roll(tile, LANES // 2, 1)
                parts = (jnp.where(lane < LANES // 2, tile, turned), jnp.where(lane < LANES // 2, turned, tile))
                for a in range(b2x):
                    part = parts[a // (b2x // 2)]
                    row = (a % (b2x // 2)) * b2y
                    fs[0][x * b2x + a, pl.ds(yb * b2y, b2y), :] = part[row: row + b2y]
        coarse(0)
        solved = dot_lanes(vs[0][...], mats[0, 1])
        for yb in range(n_yb):
            chunks[yb, :, pl.ds(0, b2y), :] = solved[:, yb * b2y:(yb + 1) * b2y]
        for a in range(2 * (WIDE // 2) + b2x):
            xa = lax.rem(ix * b2x - WIDE // 2 + a + nx2, nx2)
            for j in range(3):
                part = chunks[lax.rem(iyb + j - 1 + n_yb, n_yb), xa, pl.ds(0, b2y), :]
                window[a, pl.ds(j * b1y, b2y, stride=2), :] = part
                window[a, pl.ds(j * b1y + 1, b2y, stride=2), :] = part
        if cycle == 0:
            for copy in exchange:
                copy.wait_recv()
        top = reach - 1
        v = begin1(f1_here, top)
        first_plane, planes = WIDE - top, b1x + 2 * top
        wide = window[first_plane // 2: (first_plane + planes + 1) // 2]
        wide = jnp.broadcast_to(wide[:, None], (wide.shape[0], 2) + wide.shape[1:]).reshape((-1,) + wide.shape[1:])
        v1[span(top)] = v + wide[first_plane % 2: first_plane % 2 + planes]
        w1[span(top - 1)] = sweep1(v1, f1_here, top - 1)
        v1[span(top - 2)] = sweep1(w1, f1_here, top - 2)
        done += exchange + gather
        if last:
            correct0(va, 2)
            sweep0(va, vb, 1)
            sweep0(vb, va, 0)
        else:
            correct0(va, SENT - 1)
            sweep0(va, vb, SENT - 2)
            sweep0(vb, va, SENT - 3)
            sweep0(va, vb, SENT - 4)
            sweep0(vb, va, SENT - 5)

    def join(c, _):
        p = HALO + 4 * c
        value = jnp.concatenate([va[z, pl.ds(p, 4), pl.ds(ROWS, by), :] for z in range(2)], -1)
        value = dot_lanes(value, join_mat[...])
        staged[0, pl.ds(4 * c, 4)] = value[..., :half]
        staged[1, pl.ds(4 * c, 4)] = value[..., half:]
        return _

    lax.fori_loop(0, bx // 4, join, None)
    mine = pl.ds(pl.multiple_of(by * iz, 8), by)
    sent = pltpu.make_async_remote_copy(
        src_ref=staged.at[other], dst_ref=out_ref.at[:, mine, :], send_sem=send3.at[0], recv_sem=recv3.at[0],
        device_id=place(ix, iy * n_gz + other), device_id_type=MESH)
    sent.start()
    kept = pltpu.make_async_copy(staged.at[iz], out_ref.at[:, mine, :], recv3.at[1])
    kept.start()
    for copy in first + done:
        copy.wait_send()
    kept.wait()
    sent.wait()


def local(sizes, charge):
    n_gx, n_gy, n_gz = sizes
    bx, cy, cz = charge.shape
    by = cy // n_gz
    n_yb = n_gy * n_gz
    assert n_gz == 2 and cz == LANES and by % 16 == 0 and by // 4 * (bx // 4) == 16
    f32 = jnp.float32
    x0, r0 = bx + 2 * HALO, by + 2 * ROWS
    x1, r1 = bx // 2 + 2 * WIDE, by // 2 + 2 * WIDE
    nx2, ny2 = bx // 4 * n_gx, by // 4 * n_yb
    n_dev = n_gx * n_yb
    n_levels = LEVELS - 2
    shapes = [(nx2 >> k, max(8, ny2 >> k), LANES) for k in range(n_levels)]
    vmem = lambda *shape: pltpu.VMEM(shape, f32)
    level0 = vmem(2, x0, r0, LANES)
    nz = n_gz * cz
    scratch = [
        level0, level0, level0, level0,
        vmem(x0 // 2, r0, LANES), vmem(x0 // 2, r0, LANES),
        vmem(x1, r1, LANES), vmem(CYCLES, x1, r1, LANES), vmem(x1, r1, LANES), vmem(x1, r1, LANES),
        vmem(bx // 4, r1, LANES),
        vmem(CYCLES, n_dev, 8, LANES),
        vmem(n_yb, nx2, 8, LANES),
        vmem(bx // 4 + WIDE, r1, LANES),
        pltpu.VMEM((LEVELS - 2, 2, LANES, LANES), jnp.bfloat16),
        pltpu.VMEM((nz, nz), jnp.bfloat16), pltpu.VMEM((nz, nz), jnp.bfloat16),
        vmem(2, bx, by, LANES),
    ]
    scratch += [vmem(*s) for s in shapes] * 2
    halves = [vmem(max(1, s[0] // 2), s[1], s[2]) for s in shapes]
    scratch += halves * 2
    dma = lambda *shape: pltpu.SemaphoreType.DMA(shape)
    scratch += [dma(3, 4), dma(3, 2, 2), dma(CYCLES, 8), dma(CYCLES, 8),
                dma(CYCLES, n_dev), dma(CYCLES, n_dev), dma(1), dma(2)]
    return pl.pallas_call(
        functools.partial(kernel, sizes),
        out_shape=jax.ShapeDtypeStruct(charge.shape, f32),
        in_specs=[pl.BlockSpec(memory_space=pl.ANY)],
        out_specs=pl.BlockSpec(memory_space=pl.ANY),
        scratch_shapes=scratch,
        compiler_params=pltpu.CompilerParams(collective_id=0, has_side_effects=True),
    )(charge)


def solution(mesh):
    sizes = (mesh.shape["gx"], mesh.shape["gy"], mesh.shape["gz"])
    return jax.shard_map(
        functools.partial(local, sizes),
        mesh=mesh,
        in_specs=(P(("groups", "gx"), "gy", "gz"),),
        out_specs=P(("groups", "gx"), "gy", "gz"),
        check_vma=False,
    )
```

time: 542 us -> 52.7 us (0.10); the launches traced: 535 us -> 52.6 us
  starting transfers between devices: 180 us -> 0 us
  waiting for transfers between devices: 124 us -> 0 us
  local copies, waits for them, and re-layouts: 106 us -> 1.67 us
  other arithmetic: 86 us -> 0 us
  Pallas kernels: 0 us -> 50.9 us
  blocking collectives: 36.5 us -> 0 us
    ppermute x168 -> x0, starting transfers between devices: 180 us -> none  [the longest x84 118 us: extended(): after = lax.ppermute(leading, axis, down)]
    ppermute x168 -> x0, waiting for transfers between devices: 124 us -> none  [the longest x84 87.8 us: extended(): before = lax.ppermute(last, axis, up)]
    pallas_call x0 -> x1, Pallas kernels: none -> 50.9 us  [local(): pl.pallas_call(functools.partial(kernel, sizes), out_shape=jax.ShapeDtype...]
    reshape x20 -> x0, local copies, waits for them, and re-layouts: 45.3 us -> none  [the longest x8 43.8 us: restrict(): blocks = field.reshape(size_x // 2, 2, size_y // 2, 2, size_z // 2, 2)]
    add x58 -> x0, other arithmetic: 38 us -> none  [the longest x16 21.9 us: smooth(): wide_field[1:-1, 1:-1, 1:-1]]
    all_gather x6 -> x0, blocking collectives: 36.5 us -> none  [the longest x2 24.5 us: collect(): return lax.all_gather(slab, 'gx', axis=0, tiled=True)]
    unnamed x119 -> x1, local copies, waits for them, and re-layouts: 23.4 us -> 1.67 us
    reduce_sum x16 -> x0, other arithmetic: 18.9 us -> none  [restrict(): return blocks.mean(axis=(1, 3, 5))]
  transfers between devices with their start and end apart: 168 -> 0, of which waited for: 122 -> 0; matrix products, arithmetic and copies ran while one was open for 15% -> 0% of each run, Pallas kernels for 0% -> 0%
where the time goes in v1:
time: 52.7 us; the launch traced here: 52.6 us
  Pallas kernels  50.9 us (97%)
  local copies, waits for them, and re-layouts  1.67 us (3%)
    pallas_call x1, Pallas kernels, local(): pl.pallas_call(functools.partial(kernel, sizes), out_shape=jax.ShapeDtype...  50.9 us
    unnamed x1, local copies, waits for them, and re-layouts  1.67 us

profile of v1, /device:TPU:0, one launch (start us, length us, event | category | flops | bytes accessed | tf_op | source)
XLA Modules:
  0.0 52.6 jit_solution(5674314834448497228)
XLA Ops:
  0.0 50.9 %shard_map.17 = f32[16,32,128]{2,1,0:T(8,128)} custom-call(f32[16,32,128]{2,1,0:T(8,128)} %charge_ref.1), custom_call_target="tpu_custom_call" | custom-call | tf_op jit(solution)/shard_map/pallas_call | solution.py:424
  50.9 1.7 %copy.3 = f32[16,32,128]{2,1,0:T(8,128)} copy(f32[16,32,128]{2,1,0:T(8,128)} %shard_map.17) | data formatting | bytes 524288

commit v2 on v1

--- a/solution.py
+++ b/solution.py
@@ -98,8 +98,8 @@
     pl.semaphore_wait(barrier, len(peers))
 
     first = []
-    waits = []
-    for k, dx in enumerate((-1, 0, 1)):
+    waits = [[], [], []]
+    for k, dx in ((1, 0), (0, -1), (2, 1)):
         planes = bx if dx == 0 else SENT
         from_x = 0 if dx < 1 else bx - SENT
         to_x = {-1: HALO + bx, 0: HALO, 1: HALO - SENT}[dx]
@@ -123,10 +123,12 @@
         for z in range(n_gz):
             own = raw.at[z, pl.ds(to_x, planes), pl.ds(pl.multiple_of(ROWS * other, 8), by + ROWS), :]
             side = raw.at[z, pl.ds(to_x, planes), pl.ds(pl.multiple_of((r0 - ROWS) * iz, 8), ROWS), :]
-            waits.append(pltpu.make_async_copy(own, own, recv0.at[k, 0, z]))
-            waits.append(pltpu.make_async_copy(side, side, recv0.at[k, 1, z]))
+            waits[k].append(pltpu.make_async_copy(own, own, recv0.at[k, 0, z]))
+            waits[k].append(pltpu.make_async_copy(side, side, recv0.at[k, 1, z]))
     for copy in first:
         copy.start()
+    near = waits[1]
+    far = waits[0] + waits[2]
 
     nz = n_gz * cz
     half = nz // 2
@@ -138,21 +140,16 @@
             LANES, LANES, lambda i, j: lax.div(i, 2) == (j & (period // 2 - 1)) + jnp.where(i < period, 0, LANES))
         mats[level - 1, 1] = indicator(LANES, LANES, lambda i, j: i == lax.div(j & (period - 1), 2))
 
-    for wait in waits:
-        wait.wait()
-
-    filled = bx + 2 * SENT
-    step = max(d for d in range(1, 7) if filled % d == 0)
-
-    def deal(c, _):
-        planes = pl.ds(HALO - SENT + step * c, step)
-        value = jnp.concatenate([raw[0, planes], raw[1, planes]], -1)
-        value = dot_lanes(value, split_mat[...])
-        src[0, planes] = value[..., :half]
-        src[1, planes] = value[..., half:]
-        return _
-
-    lax.fori_loop(0, filled // step, deal, None)
+    def deal(start, count, step):
+        def body(c, _):
+            planes = pl.ds(start + step * c, step)
+            value = jnp.concatenate([raw[0, planes], raw[1, planes]], -1)
+            value = dot_lanes(value, split_mat[...])
+            src[0, planes] = value[..., :half]
+            src[1, planes] = value[..., half:]
+            return _
+
+        lax.fori_loop(0, count // step, body, None, unroll=True)
 
     def neighbours(ref, p):
         even, odd = ref[0, p], ref[1, p]
@@ -169,18 +166,18 @@
             body(p, c)
             return _
 
-        lax.fori_loop(0, (bx + 2 * extent) // 2, pair, None)
+        lax.fori_loop(0, (bx + 2 * extent) // 2, pair, None, unroll=4)
 
     scale0, diag0, alpha0, beta0 = factors(0)
 
-    def begin0(ref, extent):
-        def body(p, c):
-            for q in (p, p + 1):
-                centre, beside = neighbours(src, q)
-                for z in range(2):
-                    ref[z, q] = alpha0 * ((2.0 - OMEGA) * centre[z] + beta0 * beside[z])
-
-        over(extent, body)
+    def begin0(ref, start, count):
+        def body(c, _):
+            centre, beside = neighbours(src, start + c)
+            for z in range(2):
+                ref[z, start + c] = alpha0 * ((2.0 - OMEGA) * centre[z] + beta0 * beside[z])
+            return _
+
+        lax.fori_loop(0, count, body, None, unroll=7)
 
     def sweep0(old, new, extent):
         def body(p, c):
@@ -222,7 +219,7 @@
                     ref[z, start + 2 * c + q] = ref[z, start + 2 * c + q] + term
             return _
 
-        lax.fori_loop(0, count, body, None)
+        lax.fori_loop(0, count, body, None, unroll=2)
 
     scale1, diag1, alpha1, beta1 = factors(1)
 
@@ -274,7 +271,16 @@
 
     lane = lax.broadcasted_iota(jnp.int32, (8, LANES), 1)
     me = ix * n_yb + iyb
-    begin0(va, SENT - 1)
+    for wait in near:
+        wait.wait()
+    deal(HALO, bx, 4)
+    begin0(va, HALO + 1, bx - 2)
+    for wait in far:
+        wait.wait()
+    deal(HALO - SENT, SENT, SENT)
+    deal(HALO + bx, SENT, SENT)
+    begin0(va, HALO - SENT + 1, SENT)
+    begin0(va, HALO + bx - 1, SENT)
     done = []
     for cycle in range(CYCLES):
         last = cycle == CYCLES - 1
@@ -373,7 +379,7 @@
         staged[1, pl.ds(4 * c, 4)] = value[..., half:]
         return _
 
-    lax.fori_loop(0, bx // 4, join, None)
+    lax.fori_loop(0, bx // 4, join, None, unroll=True)
     mine = pl.ds(pl.multiple_of(by * iz, 8), by)
     sent = pltpu.make_async_remote_copy(
         src_ref=staged.at[other], dst_ref=out_ref.at[:, mine, :], send_sem=send3.at[0], recv_sem=recv3.at[0],

time: 52.7 us -> 46.3 us (0.88)
  Pallas kernels: 50.9 us -> 44.4 us
    pallas_call x1, Pallas kernels: 50.9 us -> 44.4 us  [local(): pl.pallas_call(functools.partial(kernel, sizes), out_shape=jax.ShapeDtype...]
where the time goes in v2:
time: 46.3 us; the launch traced here: 46.1 us
  Pallas kernels  44.4 us (96%)
  local copies, waits for them, and re-layouts  1.67 us (4%)
    pallas_call x1, Pallas kernels, local(): pl.pallas_call(functools.partial(kernel, sizes), out_shape=jax.ShapeDtype...  44.4 us
    unnamed x1, local copies, waits for them, and re-layouts  1.67 us

profile of v2, /device:TPU:0, one launch (start us, length us, event | category | flops | bytes accessed | tf_op | source)
XLA Modules:
  0.0 46.1 jit_solution(1218760671425250954)
XLA Ops:
  0.0 44.4 %shard_map.17 = f32[16,32,128]{2,1,0:T(8,128)} custom-call(f32[16,32,128]{2,1,0:T(8,128)} %charge_ref.1), custom_call_target="tpu_custom_call" | custom-call | tf_op jit(solution)/shard_map/pallas_call | solution.py:430
  44.5 1.7 %copy.3 = f32[16,32,128]{2,1,0:T(8,128)} copy(f32[16,32,128]{2,1,0:T(8,128)} %shard_map.17) | data formatting | bytes 524288

commit v3 on v2

--- a/solution.py
+++ b/solution.py
@@ -70,11 +70,11 @@
 
 
 def kernel(sizes, charge_ref, out_ref, raw, src, va, vb, pairs, tall, f1_local, f1, v1, w1, sum1, slots,
-           chunks, window, mats, split_mat, join_mat, staged, *rest):
+           chunks, window, mats, split_mat, join_mat, staged, beside_x, *rest):
     n_gx, n_gy, n_gz = sizes
     n_levels = LEVELS - 2
     fs, vs, ts, us = (rest[k * n_levels:(k + 1) * n_levels] for k in range(4))
-    (send0, recv0, send1, recv1, send2, recv2, send3, recv3) = rest[4 * n_levels:]
+    (send0, recv0, send1, recv1, send2, recv2, send3, recv3, send4, recv4) = rest[4 * n_levels:]
     ix, iy, iz = lax.axis_index("gx"), lax.axis_index("gy"), lax.axis_index("gz")
     bx, cy, cz = charge_ref.shape
     by = cy // n_gz
@@ -97,35 +97,44 @@
         pl.semaphore_signal(barrier, inc=1, device_id=place(ix + dx, iyb + dyb), device_id_type=MESH)
     pl.semaphore_wait(barrier, len(peers))
 
-    first = []
+    hops = []
+    first = [[], [], []]
+    local_copies = [None, None, None]
     waits = [[], [], []]
     for k, dx in ((1, 0), (0, -1), (2, 1)):
         planes = bx if dx == 0 else SENT
         from_x = 0 if dx < 1 else bx - SENT
         to_x = {-1: HALO + bx, 0: HALO, 1: HALO - SENT}[dx]
+        origin = charge_ref
+        if dx != 0:
+            origin = beside_x.at[k // 2]
+            hops.append(pltpu.make_async_remote_copy(
+                src_ref=charge_ref.at[pl.ds(from_x, planes), :, :], dst_ref=origin,
+                send_sem=send4.at[k // 2], recv_sem=recv4.at[k // 2],
+                device_id=place(ix + dx, iyb), device_id_type=MESH))
         for t, zt in enumerate((other, iz)):
             from_y = pl.multiple_of((by - ROWS) * zt, 8)
             to_y = pl.multiple_of(ROWS * (1 - zt), 8)
-            source = charge_ref.at[pl.ds(from_x, planes), pl.ds(from_y, by + ROWS), :]
+            source = origin.at[:, pl.ds(from_y, by + ROWS), :]
             target = raw.at[iz, pl.ds(to_x, planes), pl.ds(to_y, by + ROWS), :]
-            if dx == 0 and t == 1:
-                pltpu.make_async_copy(source, target, recv0.at[k, 0, iz]).start()
+            if t == 1:
+                local_copies[k] = pltpu.make_async_copy(source, target, recv0.at[k, 0, iz])
             else:
-                first.append(pltpu.make_async_remote_copy(
+                first[k].append(pltpu.make_async_remote_copy(
                     src_ref=source, dst_ref=target, send_sem=send0.at[k, t], recv_sem=recv0.at[k, 0, iz],
-                    device_id=place(ix + dx, iy * n_gz + zt), device_id_type=MESH))
+                    device_id=place(ix, iy * n_gz + zt), device_id_type=MESH))
         for t, (step, from_y, to_y) in enumerate(((-1, 0, r0 - ROWS), (n_gz, cy - ROWS, 0))):
-            first.append(pltpu.make_async_remote_copy(
-                src_ref=charge_ref.at[pl.ds(from_x, planes), pl.ds(from_y, ROWS), :],
+            first[k].append(pltpu.make_async_remote_copy(
+                src_ref=origin.at[:, pl.ds(from_y, ROWS), :],
                 dst_ref=raw.at[iz, pl.ds(to_x, planes), pl.ds(to_y, ROWS), :],
                 send_sem=send0.at[k, 2 + t], recv_sem=recv0.at[k, 1, iz],
-                device_id=place(ix + dx, iy * n_gz + step), device_id_type=MESH))
+                device_id=place(ix, iy * n_gz + step), device_id_type=MESH))
         for z in range(n_gz):
             own = raw.at[z, pl.ds(to_x, planes), pl.ds(pl.multiple_of(ROWS * other, 8), by + ROWS), :]
             side = raw.at[z, pl.ds(to_x, planes), pl.ds(pl.multiple_of((r0 - ROWS) * iz, 8), ROWS), :]
             waits[k].append(pltpu.make_async_copy(own, own, recv0.at[k, 0, z]))
             waits[k].append(pltpu.make_async_copy(side, side, recv0.at[k, 1, z]))
-    for copy in first:
+    for copy in hops + first[1] + local_copies[1:2]:
         copy.start()
     near = waits[1]
     far = waits[0] + waits[2]
@@ -166,7 +175,7 @@
             body(p, c)
             return _
 
-        lax.fori_loop(0, (bx + 2 * extent) // 2, pair, None, unroll=4)
+        lax.fori_loop(0, (bx + 2 * extent) // 2, pair, None, unroll=True)
 
     scale0, diag0, alpha0, beta0 = factors(0)
 
@@ -271,6 +280,10 @@
 
     lane = lax.broadcasted_iota(jnp.int32, (8, LANES), 1)
     me = ix * n_yb + iyb
+    for hop, k in zip(hops, (0, 2)):
+        hop.wait_recv()
+        for copy in first[k] + local_copies[k:k + 1]:
+            copy.start()
     for wait in near:
         wait.wait()
     deal(HALO, bx, 4)
@@ -387,7 +400,7 @@
     sent.start()
     kept = pltpu.make_async_copy(staged.at[iz], out_ref.at[:, mine, :], recv3.at[1])
     kept.start()
-    for copy in first + done:
+    for copy in hops + first[0] + first[1] + first[2] + done:
         copy.wait_send()
     kept.wait()
     sent.wait()
@@ -420,13 +433,14 @@
         pltpu.VMEM((LEVELS - 2, 2, LANES, LANES), jnp.bfloat16),
         pltpu.VMEM((nz, nz), jnp.bfloat16), pltpu.VMEM((nz, nz), jnp.bfloat16),
         vmem(2, bx, by, LANES),
+        vmem(2, SENT, cy, LANES),
     ]
     scratch += [vmem(*s) for s in shapes] * 2
     halves = [vmem(max(1, s[0] // 2), s[1], s[2]) for s in shapes]
     scratch += halves * 2
     dma = lambda *shape: pltpu.SemaphoreType.DMA(shape)
     scratch += [dma(3, 4), dma(3, 2, 2), dma(CYCLES, 8), dma(CYCLES, 8),
-                dma(CYCLES, n_dev), dma(CYCLES, n_dev), dma(1), dma(2)]
+                dma(CYCLES, n_dev), dma(CYCLES, n_dev), dma(1), dma(2), dma(2), dma(2)]
     return pl.pallas_call(
         functools.partial(kernel, sizes),
         out_shape=jax.ShapeDtypeStruct(charge.shape, f32),

time: 46.3 us -> 42.8 us (0.924)
  Pallas kernels: 44.4 us -> 41 us
    pallas_call x1, Pallas kernels: 44.4 us -> 41 us  [local(): pl.pallas_call(functools.partial(kernel, sizes), out_shape=jax.ShapeDtype...]
where the time goes in v3:
time: 42.8 us; the launch traced here: 42.7 us
  Pallas kernels  41 us (96%)
  local copies, waits for them, and re-layouts  1.67 us (4%)
    pallas_call x1, Pallas kernels, local(): pl.pallas_call(functools.partial(kernel, sizes), out_shape=jax.ShapeDtype...  41 us
    unnamed x1, local copies, waits for them, and re-layouts  1.67 us

profile of v3, /device:TPU:0, one launch (start us, length us, event | category | flops | bytes accessed | tf_op | source)
XLA Modules:
  0.0 42.7 jit_solution(5146016442523566861)
XLA Ops:
  0.0 41.0 %shard_map.17 = f32[16,32,128]{2,1,0:T(8,128)} custom-call(f32[16,32,128]{2,1,0:T(8,128)} %charge_ref.1), custom_call_target="tpu_custom_call" | custom-call | tf_op jit(solution)/shard_map/pallas_call | solution.py:444
  41.0 1.7 %copy.3 = f32[16,32,128]{2,1,0:T(8,128)} copy(f32[16,32,128]{2,1,0:T(8,128)} %shard_map.17) | data formatting | bytes 524288
